TPU v7x, 256 devices: a whole 4x4x8 slice. The times are simulated.
256 devices in a mesh: dom: 32 (over x_lo, z, core), kv: 8 (over y, x_hi).
Axes of the slice: x: 4 (x_hi: 2, x_lo: 2; x = x_hi * 2 + x_lo), y: 4, z: 8, core: 2. Of those that a mesh axis runs over, the one named last changes fastest.
Arguments:
- positions: float32 [3, 65536], P(None, ('dom', 'kv')), may hold values from 0 to 60
- features: bfloat16 [65536, 128], P(('dom', 'kv')), may hold values from -6 to 6
- nbr_index: int32 [65536, 64], P(('dom', 'kv')), may hold values from 0 to 4095
- nbr_count: int32 [65536], P(('dom', 'kv')), may hold values from 16 to 64
- nbr_dist: float32 [65536, 64], P(('dom', 'kv')), may hold values from 0.8 to 5
- halo_lists: int32 [32, 2, 1024], P('dom'), may hold values from 0 to 2047
- wave_vectors: float32 [3, 2048], replicated, may hold values from -1.2566371 to 1.2566371, as said below
- w_charge_first: bfloat16 [128, 16], replicated, may hold values from -0.5 to 0.5
- w_long_first: float32 [16, 128], replicated, may hold values from -1.5 to 1.5
- w_value: bfloat16 [128, 128], replicated, may hold values from -0.5 to 0.5
- w_filter: float32 [16, 128], replicated, may hold values from -1.5 to 1.5
- w_charge_second: bfloat16 [128, 16], replicated, may hold values from -0.5 to 0.5
- w_long_second: float32 [16, 128], replicated, may hold values from -1.5 to 1.5
Outputs:
- features_out: bfloat16 [65536, 128], P(('dom', 'kv'))
- forces: float32 [3, 65536], P(None, ('dom', 'kv'))
Inputs may be any that keep to these rules, and one draw needn't show every extreme that they name: `nbr_index`: rows of the atom's own domain table. `nbr_count`: slots at or past the count are padding. `halo_lists`: rows among the domain's own 2048 atoms; repeats may occur. `wave_vectors`: the columns are 2 pi n / 60 for 2048 distinct nonzero integer vectors n of smallest length, no two equal or opposite, in no particular order.
All inputs are finite; a program needn't handle non-finite values.
Results may differ from a plain program's by a relative error of at most 0.0054.
Values may be sent and summed in bfloat16 or wider, within the bound.
No kernel may reach another device: no remote copies, remote signals or barrier semaphores. Data moves between devices by JAX's collectives and lax.ppermute only.
A program may use at most 64 MiB of HBM per device.

v0:
```python
import math
import jax
import jax.numpy as jnp
from jax import lax
from jax.sharding import PartitionSpec as P

HIGHEST_PRECISION = lax.Precision.HIGHEST
LONG_SCALE = 2.0


def passed_along(block, axis, distance):
    devices = range(lax.axis_size(axis))
    route = [((i - distance) % len(devices), i) for i in devices]
    return lax.ppermute(block, axis, route)


def wave_weight(wavevec):
    sq_norm = wavevec[0] * wavevec[0] + wavevec[1] * wavevec[1] + wavevec[2] * wavevec[2]
    return jnp.exp(-0.5 * sq_norm) / (sq_norm + 1.0)


def phase_tables(wavevec, coords):
    phase_angle = (
        wavevec[0][:, None] * coords[0][None, :]
        + wavevec[1][:, None] * coords[1][None, :]
        + wavevec[2][:, None] * coords[2][None, :]
    )
    return (jnp.cos(phase_angle), jnp.sin(phase_angle))


def partial_structure(wavevec, coords, charge):
    cos_table, sin_table = phase_tables(wavevec, coords)
    return (
        jnp.dot(cos_table, charge, precision=HIGHEST_PRECISION, preferred_element_type=jnp.float32),
        jnp.dot(sin_table, charge, precision=HIGHEST_PRECISION, preferred_element_type=jnp.float32),
    )


def partial_project(wavevec, coords, charge, cos_part, sin_part):
    cos_table, sin_table = phase_tables(wavevec, coords)
    weight = wave_weight(wavevec)[:, None]
    cos_weighted = weight * cos_part
    sin_weighted = weight * sin_part
    contract_dims = (((0,), (0,)), ((), ()))
    potential = lax.dot_general(
        cos_table,
        cos_weighted,
        contract_dims,
        precision=HIGHEST_PRECISION,
        preferred_element_type=jnp.float32,
    )
    potential = potential + lax.dot_general(
        sin_table,
        sin_weighted,
        contract_dims,
        precision=HIGHEST_PRECISION,
        preferred_element_type=jnp.float32,
    )
    along_cos = jnp.dot(
        cos_weighted, charge.T, precision=HIGHEST_PRECISION, preferred_element_type=jnp.float32
    )
    along_sin = jnp.dot(
        sin_weighted, charge.T, precision=HIGHEST_PRECISION, preferred_element_type=jnp.float32
    )
    mixed = sin_table * along_cos - cos_table * along_sin
    force = jnp.dot(wavevec, mixed, precision=HIGHEST_PRECISION, preferred_element_type=jnp.float32)
    return (potential, force)


def sliced_range(pos_dom, charge_dom, wave_vectors, total_atoms, atom_dev):
    kv_count = lax.axis_size("kv")
    per_device = wave_vectors.shape[1] // kv_count
    my_waves = lax.dynamic_slice_in_dim(
        wave_vectors, lax.axis_index("kv") * per_device, per_device, 1
    )
    dom_span = pos_dom.shape[1]
    channels = charge_dom.shape[1]
    atom_block = min(512, dom_span)
    block_count = dom_span // atom_block
    coord_blocks = pos_dom.reshape(3, block_count, atom_block).transpose(1, 0, 2)
    charge_blocks = charge_dom.reshape(block_count, atom_block, channels)

    def add_sums(running, member):
        add_cos, add_sin = partial_structure(my_waves, member[0], member[1])
        return ((running[0] + add_cos, running[1] + add_sin), None)

    zero_part = jnp.zeros((per_device, channels), jnp.float32)
    (cos_part, sin_part), _ = lax.scan(
        add_sums, (zero_part, zero_part), (coord_blocks, charge_blocks)
    )
    cos_part, sin_part = lax.psum((cos_part, sin_part), "dom")
    inv_root = 1.0 / math.sqrt(total_atoms)
    cos_part = cos_part * inv_root
    sin_part = sin_part * inv_root
    prefactor = LONG_SCALE / math.sqrt(wave_vectors.shape[1])
    pieces = atom_dev * lax.axis_size("kv") // atom_dev
    coords = pos_dom.reshape(3, pieces, atom_dev).transpose(1, 0, 2)
    charges = charge_dom.reshape(pieces, atom_dev, channels)

    def one_piece(member):
        potential, force = partial_project(my_waves, member[0], member[1], cos_part, sin_part)
        return jnp.concatenate([potential, force.T], axis=1) * prefactor

    summed = lax.psum_scatter(
        lax.map(one_piece, (coords, charges)).reshape(atom_dev * lax.axis_size("kv"), channels + 3),
        "kv",
        scatter_dimension=0,
        tiled=True,
    )
    return (summed[:, :channels], summed[:, channels:].T)


def basis_of(distance, live_count, basis_count):
    centers = 0.5 + 4.5 / (basis_count - 1) * jnp.arange(basis_count, dtype=jnp.int32).astype(
        jnp.float32
    )
    sharpness = ((basis_count - 1) / 4.5) ** 2
    envelope = 0.5 * (jnp.cos(math.pi * distance / 5.0) + 1.0)
    in_list = (
        jnp.arange(distance.shape[1], dtype=jnp.int32)[None, :] < live_count[:, None]
    ).astype(jnp.float32)
    radial = jnp.exp(-sharpness * (distance[..., None] - centers) ** 2)
    return (radial * (envelope * in_list)[..., None]).astype(jnp.bfloat16)


def short_range(hidden, w_value, w_filter, nbr_index, nbr_count, nbr_dist, halo_lists):
    values = jnp.dot(hidden, w_value, preferred_element_type=jnp.float32).astype(jnp.bfloat16)
    v_dom = lax.all_gather(values, "kv", axis=0, tiled=True)
    halo_rows = halo_lists[0]
    from_below = passed_along(v_dom[halo_rows[0]], "dom", 1)
    from_above = passed_along(v_dom[halo_rows[1]], "dom", -1)
    value_table = jnp.concatenate([v_dom, from_below, from_above], axis=0)
    atom_dev = hidden.shape[0]
    neigh_slots = nbr_index.shape[1]
    atom_block = min(64, atom_dev)
    block_count = atom_dev // atom_block

    def one_block(member):
        index_rows, count_rows, dist_rows = member
        picked = value_table[index_rows]
        basis = basis_of(dist_rows, count_rows, w_filter.shape[0])
        contracted = jnp.einsum("ajr,ajf->arf", basis, picked, preferred_element_type=jnp.float32)
        return jnp.einsum("arf,rf->af", contracted, w_filter, precision=HIGHEST_PRECISION)

    message = lax.map(
        one_block,
        (
            nbr_index.reshape(block_count, atom_block, neigh_slots),
            nbr_count.reshape(block_count, atom_block),
            nbr_dist.reshape(block_count, atom_block, neigh_slots),
        ),
    ).reshape(atom_dev, -1)
    return (hidden.astype(jnp.float32) + jax.nn.silu(message)).astype(jnp.bfloat16)


def local(
    positions,
    features,
    nbr_index,
    nbr_count,
    nbr_dist,
    halo_lists,
    wave_vectors,
    w_charge_first,
    w_long_first,
    w_value,
    w_filter,
    w_charge_second,
    w_long_second,
):
    atom_dev = features.shape[0]
    total_atoms = atom_dev * lax.axis_size("dom") * lax.axis_size("kv")
    charge_first = jnp.dot(features, w_charge_first, preferred_element_type=jnp.float32)
    pos_dom, charge_dom = (
        lax.all_gather(positions, "kv", axis=1, tiled=True),
        lax.all_gather(charge_first, "kv", axis=0, tiled=True),
    )
    pot_first, force_first = sliced_range(pos_dom, charge_dom, wave_vectors, total_atoms, atom_dev)
    lifted = jnp.dot(
        pot_first, w_long_first, precision=HIGHEST_PRECISION, preferred_element_type=jnp.float32
    )
    hidden_first = (features.astype(jnp.float32) + jax.nn.silu(lifted)).astype(jnp.bfloat16)
    hidden_second = short_range(
        hidden_first, w_value, w_filter, nbr_index, nbr_count, nbr_dist, halo_lists
    )
    charge_second = jnp.dot(hidden_second, w_charge_second, preferred_element_type=jnp.float32)
    charge_dom = lax.all_gather(charge_second, "kv", axis=0, tiled=True)
    pot_second, force_second = sliced_range(
        pos_dom, charge_dom, wave_vectors, total_atoms, atom_dev
    )
    lifted = jnp.dot(
        pot_second, w_long_second, precision=HIGHEST_PRECISION, preferred_element_type=jnp.float32
    )
    features_out = (hidden_second.astype(jnp.float32) + jax.nn.silu(lifted)).astype(jnp.bfloat16)
    return (features_out, force_first + force_second)


def solution(mesh):
    return jax.shard_map(
        local,
        mesh=mesh,
        in_specs=(
            P(None, ("dom", "kv")),
            P(("dom", "kv"), None),
            P(("dom", "kv"), None),
            P(("dom", "kv")),
            P(("dom", "kv"), None),
            P("dom", None, None),
            P(),
            P(),
            P(),
            P(),
            P(),
            P(),
            P(),
        ),
        out_specs=(P(("dom", "kv"), None), P(None, ("dom", "kv"))),
        check_vma=False,
    )
```

profile of v0, /device:TPU:32, one launch (start us, length us, event | category | flops | bytes accessed | tf_op | source)
XLA Modules:
  0.0 708.0 jit_solution(5735712428069415658)
XLA Ops:
  7.3 34.8 %all_gather.12 = f32[3,2048]{1,0:T(4,128)S(1)} all-gather(f32[3,256]{1,0:T(4,128)} %param.23), channel_id=1, replica_groups=mesh['dom'=32,'kv'=8] {'kv'}, dimensions={1}, use_global_device_ids=true | all-gather | bytes 27648 | tf_op jit(solution)/shard_map/all_gather | solution.py:175
  43.0 34.3 %all_gather.13 = f32[2048,16]{0,1:T(8,128)S(1)} all-gather(f32[256,16]{0,1:T(8,128)S(1)} %fusion.105), channel_id=1, replica_groups=mesh['dom'=32,'kv'=8] {'kv'}, dimensions={0}, use_global_device_ids=true | all-gather | bytes 147456 | tf_op jit(solution)/shard_map/all_gather | solution.py:176
  78.1 19.2 %while.65 = (s32[]{:T(128)}, f32[256,16]{0,1:T(8,128)S(1)}, f32[256,16]{0,1:T(8,128)S(1)}, f32[3,256]{1,0:T(4,128)S(1)}, f32[4,3,512]{2,1,0:T(4,128)S(1)}, /*ind...) while((s32[]{:T(128)}, f32[256,16]{0,1:T(8,128)S(1)}, f32[256,16]{0,1:T(8,128)S(1)}, ...), condition=%wide.region_1.2_spmd.clone, body=%wide.region_0.1_spmd.clone.sunk | while | flops 51658756 | bytes 233624 | solution.py:88
  78.2 2.4 convolution_add_fusion.11
  80.6 2.4 convolution_add_fusion.10
  83.0 2.4 convolution_add_fusion.11
  85.4 2.4 convolution_add_fusion.10
  87.8 2.4 convolution_add_fusion.11
  90.2 2.4 convolution_add_fusion.10
  92.6 2.4 convolution_add_fusion.11
  95.0 2.4 convolution_add_fusion.10
  97.4 103.2 %all-reduce.1 = (f32[256,16]{0,1:T(8,128)S(1)}, f32[256,16]{0,1:T(8,128)S(1)}) all-reduce(f32[256,16]{0,1:T(8,128)S(1)} %get-tuple-element.339, f32[256,16]{0,1:T(8,128)S(1)} %get-tuple-element.340), channel_id=1, replica_groups=mesh['dom'=32,'kv'=8] {'dom'}, use_global_device_ids=true, to_apply=%region_2.3 | all-reduce | flops 8192 | bytes 65536 | tf_op jit(solution)/shard_map/psum | solution.py:91
  201.5 43.6 %while.62 = (s32[]{:T(128)}, f32[8,256,19]{1,0,2:T(8,128)S(1)}, f32[3,256]{1,0:T(4,128)S(1)}, f32[8,3,256]{2,1,0:T(4,128)S(1)}, f32[256,1]{0,1:T(1,128)S(1)}, /*...) while((s32[]{:T(128)}, f32[8,256,19]{1,0,2:T(8,128)S(1)}, ...), condition=%wide.region_5.6_spmd, body=%wide.region_4.5_spmd.sunk | while | flops 54229252 | bytes 1394849 | solution.py:105
  201.6 1.3 convolution_multiply_fusion.6
  208.3 1.3 fusion.162
  213.8 1.3 fusion.162
  218.0 1.3 convolution_multiply_fusion.6
  219.2 1.3 fusion.162
  223.4 1.3 convolution_multiply_fusion.6
  224.7 1.3 fusion.162
  228.8 1.3 convolution_multiply_fusion.6
  230.1 1.3 fusion.162
  235.6 1.3 fusion.162
  239.7 1.3 convolution_multiply_fusion.6
  241.0 1.3 fusion.162
  246.0 75.5 %reduce-scatter.3.cloned.1.call-done = f32[256,19]{0,1:T(8,128)} async-done(((f32[2048,19]{0,1:T(8,128)}), f32[256,19]{0,1:T(8,128)}) %reduce-scatter.3.cloned.1.call-update) | async-done | bytes 19472 | tf_op jit(solution)/shard_map/reduce_scatter | solution.py:104
  322.8 36.1 %all_gather.14 = bf16[2048,128]{1,0:T(8,128)(2,1)S(1)} all-gather(bf16[256,128]{1,0:T(8,128)(2,1)S(1)} %convolution_convert_fusion), channel_id=1, replica_groups=mesh['dom'=32,'kv'=8] {'kv'}, dimensions={0}, use_global_device_ids=true | all-gather | bytes 589824 | tf_op jit(solution)/shard_map/all_gather | solution.py:128
  359.0 3.2 gather_fusion.1
  362.5 3.2 gather_fusion.2
  365.7 1.8 collective-permute-start.1
  368.3 3.1 collective-permute-done.1
  371.5 51.7 %while.63 = (s32[]{:T(128)}, f32[4,64,128]{2,1,0:T(8,128)S(1)}, f32[4,64,64]{2,1,0:T(8,128)S(1)}, s32[4,64]{1,0:T(4,128)S(1)}, s32[4,64,64]{2,1,0:T(8,128)S(1)},...) while((s32[]{:T(128)}, f32[4,64,128]{2,1,0:T(8,128)S(1)}, ...), condition=%wide.region_8.9_spmd, body=%wide.region_7.8_spmd.sunk | while | flops 17395760 | bytes 3449829 | solution.py:145
  371.8 12.1 %gather_fusion = bf16[4096,128]{1,0:T(8,128)(2,1)S(1)} fusion(bf16[4096,128]{1,0:T(8,128)(2,1)S(1)} %get-tuple-element.930, s32[4096]{0:T(1024)S(1)} %broadcast_clamp_fusion.4), kind=kCustom, calls=%fused_computation.clone.1 | custom fusion | bytes 2113536 | tf_op jit(solution)/shard_map/while/body/eval_jaxpr/gather | solution.py:140
  384.7 12.1 %gather_fusion = bf16[4096,128]{1,0:T(8,128)(2,1)S(1)} fusion(bf16[4096,128]{1,0:T(8,128)(2,1)S(1)} %get-tuple-element.930, s32[4096]{0:T(1024)S(1)} %broadcast_clamp_fusion.4), kind=kCustom, calls=%fused_computation.clone.1 | custom fusion | bytes 2113536 | tf_op jit(solution)/shard_map/while/body/eval_jaxpr/gather | solution.py:140
  397.6 12.1 %gather_fusion = bf16[4096,128]{1,0:T(8,128)(2,1)S(1)} fusion(bf16[4096,128]{1,0:T(8,128)(2,1)S(1)} %get-tuple-element.930, s32[4096]{0:T(1024)S(1)} %broadcast_clamp_fusion.4), kind=kCustom, calls=%fused_computation.clone.1 | custom fusion | bytes 2113536 | tf_op jit(solution)/shard_map/while/body/eval_jaxpr/gather | solution.py:140
  410.5 12.1 %gather_fusion = bf16[4096,128]{1,0:T(8,128)(2,1)S(1)} fusion(bf16[4096,128]{1,0:T(8,128)(2,1)S(1)} %get-tuple-element.930, s32[4096]{0:T(1024)S(1)} %broadcast_clamp_fusion.4), kind=kCustom, calls=%fused_computation.clone.1 | custom fusion | bytes 2113536 | tf_op jit(solution)/shard_map/while/body/eval_jaxpr/gather | solution.py:140
  423.4 34.5 %all_gather.15 = f32[2048,16]{0,1:T(8,128)S(1)} all-gather(f32[256,16]{0,1:T(8,128)S(1)} %fusion.106), channel_id=1, replica_groups=mesh['dom'=32,'kv'=8] {'kv'}, dimensions={0}, use_global_device_ids=true | all-gather | bytes 147456 | tf_op jit(solution)/shard_map/all_gather | solution.py:187
  458.0 19.2 %while.66 = (s32[]{:T(128)}, f32[256,16]{0,1:T(8,128)S(1)}, f32[256,16]{0,1:T(8,128)S(1)}, f32[3,256]{1,0:T(4,128)S(1)}, f32[4,3,512]{2,1,0:T(4,128)S(1)}, /*ind...) while((s32[]{:T(128)}, f32[256,16]{0,1:T(8,128)S(1)}, ...), condition=%wide.region_10.11_spmd.clone, body=%wide.region_9.10_spmd.clone.sunk | while | flops 51658756 | bytes 233624 | solution.py:88
  458.1 2.4 convolution_add_fusion.13
  460.5 2.4 convolution_add_fusion.12
  462.9 2.4 convolution_add_fusion.13
  465.3 2.4 convolution_add_fusion.12
  467.7 2.4 convolution_add_fusion.13
  470.1 2.4 convolution_add_fusion.12
  472.6 2.4 convolution_add_fusion.13
  474.9 2.4 convolution_add_fusion.12
  477.3 102.6 %all-reduce = (f32[256,16]{0,1:T(8,128)S(1)}, f32[256,16]{0,1:T(8,128)S(1)}) all-reduce(f32[256,16]{0,1:T(8,128)S(1)} %get-tuple-element.343, f32[256,16]{0,1:T(8,128)S(1)} %get-tuple-element.344), channel_id=1, replica_groups=mesh['dom'=32,'kv'=8] {'dom'}, use_global_device_ids=true, to_apply=%region_11.12 | all-reduce | flops 8192 | bytes 65536 | tf_op jit(solution)/shard_map/psum | solution.py:91
  580.0 43.6 %while.64 = (s32[]{:T(128)}, f32[8,256,19]{1,0,2:T(8,128)S(1)}, f32[3,256]{1,0:T(4,128)S(1)}, f32[8,3,256]{2,1,0:T(4,128)S(1)}, f32[256,1]{0,1:T(1,128)S(1)}, /*...) while((s32[]{:T(128)}, f32[8,256,19]{1,0,2:T(8,128)S(1)}, ...), condition=%wide.region_14.15_spmd, body=%wide.region_13.14_spmd.sunk | while | flops 54229252 | bytes 1394849 | solution.py:105
  586.8 1.3 fusion.177
  591.0 1.3 convolution_multiply_fusion.7
  592.2 1.3 fusion.177
  596.4 1.3 convolution_multiply_fusion.7
  597.7 1.3 fusion.177
  601.9 1.3 convolution_multiply_fusion.7
  603.1 1.3 fusion.177
  607.3 1.3 convolution_multiply_fusion.7
  608.6 1.3 fusion.177
  612.8 1.3 convolution_multiply_fusion.7
  614.0 1.3 fusion.177
  618.2 1.3 convolution_multiply_fusion.7
  619.5 1.3 fusion.177
  624.4 73.8 %reduce-scatter.5.cloned.1.call-done = f32[256,19]{0,1:T(8,128)} async-done(((f32[2048,19]{0,1:T(8,128)}), f32[256,19]{0,1:T(8,128)}) %reduce-scatter.5.cloned.1.call-update) | async-done | bytes 19472 | tf_op jit(solution)/shard_map/reduce_scatter | solution.py:104
  698.1 1.3 fusion.97
  699.4 1.8 add_convert_fusion
  (281 shorter events, 64.5 us)
Async XLA Ops:
  7.2 315.5 %copy-start = (bf16[128,128]{1,0:T(8,128)(2,1)S(1)}, bf16[128,128]{1,0:T(8,128)(2,1)}, u32[]{:S(2)}) copy-start(bf16[128,128]{1,0:T(8,128)(2,1)} %param.32) | copy-start | bytes 98308
  7.2 314.4 %reduce-scatter.3.cloned.1.call-start = ((), (), s32[]{:S(2)}) async-start(), calls=%async_computation.2 | async-start | bytes 221184 | tf_op jit(solution)/shard_map/reduce_scatter | solution.py:104
  201.5 44.4 %copy-start.4 = (s32[1,2,1024]{2,1,0:T(2,128)S(1)}, s32[1,2,1024]{2,1,0:T(2,128)}, u32[]{:S(2)}) copy-start(s32[1,2,1024]{2,1,0:T(2,128)} %param.28) | copy-start | bytes 24580
  201.5 120.0 %copy-start.3 = (bf16[256,128]{1,0:T(8,128)(2,1)S(1)}, bf16[256,128]{1,0:T(8,128)(2,1)}, u32[]{:S(2)}) copy-start(bf16[256,128]{1,0:T(8,128)(2,1)} %param.24) | copy-start | bytes 196612
  201.5 120.0 %copy-start.7 = (f32[16,128]{1,0:T(8,128)S(1)}, f32[16,128]{1,0:T(8,128)}, u32[]{:S(2)}) copy-start(f32[16,128]{1,0:T(8,128)} %param.31) | copy-start | bytes 24580
  245.9 452.2 %reduce-scatter.5.cloned.1.call-start = ((), (), s32[]{:S(2)}) async-start(), calls=%async_computation.3 | async-start | bytes 221184 | tf_op jit(solution)/shard_map/reduce_scatter | solution.py:104
  362.2 5.3 copy-start.1
  362.2 5.4 copy-start.2
  362.2 5.5 copy-start.6
  362.2 6.1 collective-permute-start
  365.7 5.7 collective-permute-start.1
  367.8 3.7 copy-start.8
  371.5 51.8 %copy-start.5 = (bf16[128,16]{0,1:T(8,128)(2,1)S(1)}, bf16[128,16]{0,1:T(8,128)(2,1)}, u32[]{:S(2)}) copy-start(bf16[128,16]{0,1:T(8,128)(2,1)} %param.34) | copy-start | bytes 12292
  580.0 119.4 %copy-start.9 = (f32[16,128]{1,0:T(8,128)S(1)}, f32[16,128]{1,0:T(8,128)}, u32[]{:S(2)}) copy-start(f32[16,128]{1,0:T(8,128)} %param.35) | copy-start | bytes 24580
Sparse Core Ops, SparseCore 0:
  246.0 75.4 reduce-scatter.2
  624.5 73.5 reduce-scatter.4
where the time goes:
time: 709 us; the launch traced here: 708 us
  blocking collectives  346 us (49%)
  waiting for transfers between devices  153 us (22%)
  matrix products  126 us (18%)
  local copies, waits for them, and re-layouts  61 us (9%)
  between operations  14.4 us (2%)
    psum x2, blocking collectives, sliced_range(): cos_part, sin_part = lax.psum((cos_part, sin_part), 'dom')  206 us
    reduce_scatter x2, waiting for transfers between devices, sliced_range(): lax.psum_scatter(lax.map(one_piece, (coords, charges)).reshape(atom_dev *...  149 us
    gather x4, local copies, waits for them, and re-layouts, one_block(): picked = value_table[index_rows]  48.5 us
    all_gather x1, blocking collectives, short_range(): v_dom = lax.all_gather(values, 'kv', axis=0, tiled=True)  36.1 us
    all_gather x1, blocking collectives, local(): lax.all_gather(positions, 'kv', axis=1, tiled=True)  34.8 us
    all_gather x1, blocking collectives, local(): charge_dom = lax.all_gather(charge_second, 'kv', axis=0, tiled=True)  34.5 us
    all_gather x1, blocking collectives, local(): lax.all_gather(charge_first, 'kv', axis=0, tiled=True)  34.3 us
    dot_general x16, matrix products, partial_project(): jnp.dot(sin_weighted, charge.T, precision=HIGHEST_PRECISION, preferred_el...  20.2 us
  transfers between devices with their start and end apart: 4, of which 4 were waited for; matrix products, arithmetic and copies ran while one was open for 0% of the time, Pallas kernels for 0%

commit v1 on v0

--- a/solution.py
+++ b/solution.py
@@ -125,7 +125,9 @@
 
 def short_range(hidden, w_value, w_filter, nbr_index, nbr_count, nbr_dist, halo_lists):
     values = jnp.dot(hidden, w_value, preferred_element_type=jnp.float32).astype(jnp.bfloat16)
-    v_dom = lax.all_gather(values, "kv", axis=0, tiled=True)
+    v_dom = jnp.concatenate(
+        lax.all_to_all(jnp.stack([values] * lax.axis_size("kv")), "kv", 0, 0), axis=0
+    )
     halo_rows = halo_lists[0]
     from_below = passed_along(v_dom[halo_rows[0]], "dom", 1)
     from_above = passed_along(v_dom[halo_rows[1]], "dom", -1)

time: 709 us -> 687 us (0.969)
  blocking collectives: 346 us -> 310 us
  waiting for transfers between devices: 153 us -> 161 us
    all_gather x1 -> x0, blocking collectives: 36.1 us -> none  [short_range(): v_dom = lax.all_gather(values, 'kv', axis=0, tiled=True)]
    all_to_all x0 -> x1, waiting for transfers between devices: none -> 10.1 us  [short_range(): lax.all_to_all(jnp.stack([values] * lax.axis_size('kv')), 'kv', 0, 0)]
  transfers between devices with their start and end apart: 4 -> 5, of which waited for: 4 -> 5; matrix products, arithmetic and copies ran while one was open for 0% -> 1% of each run, Pallas kernels for 0% -> 0%
where the time goes in v1:
time: 687 us; the launch traced here: 686 us
  blocking collectives  310 us (45%)
  waiting for transfers between devices  161 us (23%)
  matrix products  126 us (18%)
  local copies, waits for them, and re-layouts  61.9 us (9%)
  between operations  14.4 us (2%)
    psum x2, blocking collectives, sliced_range(): cos_part, sin_part = lax.psum((cos_part, sin_part), 'dom')  206 us
    reduce_scatter x2, waiting for transfers between devices, sliced_range(): lax.psum_scatter(lax.map(one_piece, (coords, charges)).reshape(atom_dev *...  148 us
    gather x4, local copies, waits for them, and re-layouts, one_block(): picked = value_table[index_rows]  48.5 us
    all_gather x1, blocking collectives, local(): lax.all_gather(positions, 'kv', axis=1, tiled=True)  34.8 us
    all_gather x1, blocking collectives, local(): charge_dom = lax.all_gather(charge_second, 'kv', axis=0, tiled=True)  34.5 us
    all_gather x1, blocking collectives, local(): lax.all_gather(charge_first, 'kv', axis=0, tiled=True)  34.3 us
    dot_general x16, matrix products, partial_project(): jnp.dot(sin_weighted, charge.T, precision=HIGHEST_PRECISION, preferred_el...  20.2 us
    dot_general x16, matrix products, partial_project(): jnp.dot(cos_weighted, charge.T, precision=HIGHEST_PRECISION, preferred_el...  20.1 us
  transfers between devices with their start and end apart: 5, of which 5 were waited for; matrix products, arithmetic and copies ran while one was open for 1% of the time, Pallas kernels for 0%

profile of v1, /device:TPU:32, one launch (start us, length us, event | category | flops | bytes accessed | tf_op | source)
XLA Modules:
  0.0 686.0 jit_solution(12406816517072095136)
XLA Ops:
  7.3 34.8 %all_gather.9 = f32[3,2048]{1,0:T(4,128)S(1)} all-gather(f32[3,256]{1,0:T(4,128)} %param.23), channel_id=1, replica_groups=mesh['dom'=32,'kv'=8] {'kv'}, dimensions={1}, use_global_device_ids=true | all-gather | bytes 27648 | tf_op jit(solution)/shard_map/all_gather | solution.py:177
  43.0 34.3 %all_gather.10 = f32[2048,16]{0,1:T(8,128)S(1)} all-gather(f32[256,16]{0,1:T(8,128)S(1)} %fusion.105), channel_id=1, replica_groups=mesh['dom'=32,'kv'=8] {'kv'}, dimensions={0}, use_global_device_ids=true | all-gather | bytes 147456 | tf_op jit(solution)/shard_map/all_gather | solution.py:178
  78.1 19.2 %while.65 = (s32[]{:T(128)}, f32[256,16]{0,1:T(8,128)S(1)}, f32[256,16]{0,1:T(8,128)S(1)}, f32[3,256]{1,0:T(4,128)S(1)}, f32[4,3,512]{2,1,0:T(4,128)S(1)}, /*ind...) while((s32[]{:T(128)}, f32[256,16]{0,1:T(8,128)S(1)}, f32[256,16]{0,1:T(8,128)S(1)}, ...), condition=%wide.region_1.2_spmd.clone, body=%wide.region_0.1_spmd.clone.sunk | while | flops 51658756 | bytes 233624 | solution.py:88
  78.2 2.4 convolution_add_fusion.11
  80.6 2.4 convolution_add_fusion.10
  83.0 2.4 convolution_add_fusion.11
  85.4 2.4 convolution_add_fusion.10
  87.8 2.4 convolution_add_fusion.11
  90.2 2.4 convolution_add_fusion.10
  92.6 2.4 convolution_add_fusion.11
  95.0 2.4 convolution_add_fusion.10
  97.4 103.2 %all-reduce.1 = (f32[256,16]{0,1:T(8,128)S(1)}, f32[256,16]{0,1:T(8,128)S(1)}) all-reduce(f32[256,16]{0,1:T(8,128)S(1)} %get-tuple-element.339, f32[256,16]{0,1:T(8,128)S(1)} %get-tuple-element.340), channel_id=1, replica_groups=mesh['dom'=32,'kv'=8] {'dom'}, use_global_device_ids=true, to_apply=%region_2.3 | all-reduce | flops 8192 | bytes 65536 | tf_op jit(solution)/shard_map/psum | solution.py:91
  201.5 43.6 %while.62 = (s32[]{:T(128)}, f32[8,256,19]{1,0,2:T(8,128)S(1)}, f32[3,256]{1,0:T(4,128)S(1)}, f32[8,3,256]{2,1,0:T(4,128)S(1)}, f32[256,1]{0,1:T(1,128)S(1)}, /*...) while((s32[]{:T(128)}, f32[8,256,19]{1,0,2:T(8,128)S(1)}, ...), condition=%wide.region_5.6_spmd, body=%wide.region_4.5_spmd.sunk | while | flops 54229252 | bytes 1394849 | solution.py:105
  202.9 1.3 fusion.162
  208.3 1.3 fusion.162
  212.5 1.3 convolution_multiply_fusion.6
  213.8 1.3 fusion.162
  219.2 1.3 fusion.162
  224.6 1.3 fusion.162
  228.8 1.3 convolution_multiply_fusion.6
  230.1 1.3 fusion.162
  235.5 1.3 fusion.162
  241.0 1.3 fusion.162
  245.9 75.7 %reduce-scatter.3.cloned.1.call-done = f32[256,19]{0,1:T(8,128)} async-done(((f32[2048,19]{0,1:T(8,128)}), f32[256,19]{0,1:T(8,128)}) %reduce-scatter.3.cloned.1.call-update) | async-done | bytes 19472 | tf_op jit(solution)/shard_map/reduce_scatter | solution.py:104
  323.7 4.5 all-to-all-start
  328.4 10.1 %all-to-all-done = bf16[8,256,128]{2,1,0:T(8,128)(2,1)S(1)} async-done(((bf16[8,256,128]{2,1,0:T(8,128)(2,1)}), bf16[8,256,128]{2,1,0:T(8,128)(2,1)S(1)}, u32[]{:S(2)}, u32[]{:S(2)}) %all-to-all-start) | async-done | bytes 524320 | tf_op jit(solution)/shard_map/all_to_all | solution.py:129
  338.5 3.2 gather_fusion.1
  342.0 3.2 gather_fusion.2
  345.2 1.8 collective-permute-start.1
  347.8 3.1 collective-permute-done.1
  351.0 51.7 %while.63 = (s32[]{:T(128)}, f32[4,64,128]{2,1,0:T(8,128)S(1)}, f32[4,64,64]{2,1,0:T(8,128)S(1)}, s32[4,64]{1,0:T(4,128)S(1)}, s32[4,64,64]{2,1,0:T(8,128)S(1)},...) while((s32[]{:T(128)}, f32[4,64,128]{2,1,0:T(8,128)S(1)}, ...), condition=%wide.region_8.9_spmd, body=%wide.region_7.8_spmd.sunk | while | flops 17395760 | bytes 3449829 | solution.py:147
  351.3 12.1 %gather_fusion = bf16[4096,128]{1,0:T(8,128)(2,1)S(1)} fusion(bf16[4096,128]{1,0:T(8,128)(2,1)S(1)} %get-tuple-element.930, s32[4096]{0:T(1024)S(1)} %broadcast_clamp_fusion.4), kind=kCustom, calls=%fused_computation.clone.1 | custom fusion | bytes 2113536 | tf_op jit(solution)/shard_map/while/body/eval_jaxpr/gather | solution.py:142
  364.2 12.1 %gather_fusion = bf16[4096,128]{1,0:T(8,128)(2,1)S(1)} fusion(bf16[4096,128]{1,0:T(8,128)(2,1)S(1)} %get-tuple-element.930, s32[4096]{0:T(1024)S(1)} %broadcast_clamp_fusion.4), kind=kCustom, calls=%fused_computation.clone.1 | custom fusion | bytes 2113536 | tf_op jit(solution)/shard_map/while/body/eval_jaxpr/gather | solution.py:142
  377.1 12.1 %gather_fusion = bf16[4096,128]{1,0:T(8,128)(2,1)S(1)} fusion(bf16[4096,128]{1,0:T(8,128)(2,1)S(1)} %get-tuple-element.930, s32[4096]{0:T(1024)S(1)} %broadcast_clamp_fusion.4), kind=kCustom, calls=%fused_computation.clone.1 | custom fusion | bytes 2113536 | tf_op jit(solution)/shard_map/while/body/eval_jaxpr/gather | solution.py:142
  390.0 12.1 %gather_fusion = bf16[4096,128]{1,0:T(8,128)(2,1)S(1)} fusion(bf16[4096,128]{1,0:T(8,128)(2,1)S(1)} %get-tuple-element.930, s32[4096]{0:T(1024)S(1)} %broadcast_clamp_fusion.4), kind=kCustom, calls=%fused_computation.clone.1 | custom fusion | bytes 2113536 | tf_op jit(solution)/shard_map/while/body/eval_jaxpr/gather | solution.py:142
  402.9 34.5 %all_gather.11 = f32[2048,16]{0,1:T(8,128)S(1)} all-gather(f32[256,16]{0,1:T(8,128)S(1)} %fusion.106), channel_id=1, replica_groups=mesh['dom'=32,'kv'=8] {'kv'}, dimensions={0}, use_global_device_ids=true | all-gather | bytes 147456 | tf_op jit(solution)/shard_map/all_gather | solution.py:189
  437.5 19.2 %while.66 = (s32[]{:T(128)}, f32[256,16]{0,1:T(8,128)S(1)}, f32[256,16]{0,1:T(8,128)S(1)}, f32[3,256]{1,0:T(4,128)S(1)}, f32[4,3,512]{2,1,0:T(4,128)S(1)}, /*ind...) while((s32[]{:T(128)}, f32[256,16]{0,1:T(8,128)S(1)}, ...), condition=%wide.region_10.11_spmd.clone, body=%wide.region_9.10_spmd.clone.sunk | while | flops 51658756 | bytes 233624 | solution.py:88
  437.6 2.4 convolution_add_fusion.13
  439.9 2.4 convolution_add_fusion.12
  442.4 2.4 convolution_add_fusion.13
  444.7 2.4 convolution_add_fusion.12
  447.2 2.4 convolution_add_fusion.13
  449.5 2.4 convolution_add_fusion.12
  452.0 2.4 convolution_add_fusion.13
  454.4 2.4 convolution_add_fusion.12
  456.7 102.8 %all-reduce = (f32[256,16]{0,1:T(8,128)S(1)}, f32[256,16]{0,1:T(8,128)S(1)}) all-reduce(f32[256,16]{0,1:T(8,128)S(1)} %get-tuple-element.343, f32[256,16]{0,1:T(8,128)S(1)} %get-tuple-element.344), channel_id=1, replica_groups=mesh['dom'=32,'kv'=8] {'dom'}, use_global_device_ids=true, to_apply=%region_11.12 | all-reduce | flops 8192 | bytes 65536 | tf_op jit(solution)/shard_map/psum | solution.py:91
  559.6 43.6 %while.64 = (s32[]{:T(128)}, f32[8,256,19]{1,0,2:T(8,128)S(1)}, f32[3,256]{1,0:T(4,128)S(1)}, f32[8,3,256]{2,1,0:T(4,128)S(1)}, f32[256,1]{0,1:T(1,128)S(1)}, /*...) while((s32[]{:T(128)}, f32[8,256,19]{1,0,2:T(8,128)S(1)}, ...), condition=%wide.region_14.15_spmd, body=%wide.region_13.14_spmd.sunk | while | flops 54229252 | bytes 1394849 | solution.py:105
  559.7 1.3 convolution_multiply_fusion.7
  566.4 1.3 fusion.177
  570.6 1.3 convolution_multiply_fusion.7
  571.9 1.3 fusion.177
  576.1 1.3 convolution_multiply_fusion.7
  577.3 1.3 fusion.177
  581.5 1.3 convolution_multiply_fusion.7
  582.8 1.3 fusion.177
  587.0 1.3 convolution_multiply_fusion.7
  588.2 1.3 fusion.177
  592.4 1.3 convolution_multiply_fusion.7
  593.7 1.3 fusion.177
  597.9 1.3 convolution_multiply_fusion.7
  599.1 1.3 fusion.177
  604.0 72.1 %reduce-scatter.5.cloned.1.call-done = f32[256,19]{0,1:T(8,128)} async-done(((f32[2048,19]{0,1:T(8,128)}), f32[256,19]{0,1:T(8,128)}) %reduce-scatter.5.cloned.1.call-update) | async-done | bytes 19472 | tf_op jit(solution)/shard_map/reduce_scatter | solution.py:104
  676.1 1.3 fusion.97
  677.4 1.8 add_convert_fusion
  (283 shorter events, 66.6 us)
Async XLA Ops:
  7.2 315.5 %copy-start = (bf16[128,128]{1,0:T(8,128)(2,1)S(1)}, bf16[128,128]{1,0:T(8,128)(2,1)}, u32[]{:S(2)}) copy-start(bf16[128,128]{1,0:T(8,128)(2,1)} %param.32) | copy-start | bytes 98308
  7.2 314.4 %reduce-scatter.3.cloned.1.call-start = ((), (), s32[]{:S(2)}) async-start(), calls=%async_computation.3 | async-start | bytes 221184 | tf_op jit(solution)/shard_map/reduce_scatter | solution.py:104
  201.5 120.0 %copy-start.3 = (bf16[256,128]{1,0:T(8,128)(2,1)S(1)}, bf16[256,128]{1,0:T(8,128)(2,1)}, u32[]{:S(2)}) copy-start(bf16[256,128]{1,0:T(8,128)(2,1)} %param.24) | copy-start | bytes 196612
  201.5 120.0 %copy-start.7 = (f32[16,128]{1,0:T(8,128)S(1)}, f32[16,128]{1,0:T(8,128)}, u32[]{:S(2)}) copy-start(f32[16,128]{1,0:T(8,128)} %param.31) | copy-start | bytes 24580
  322.7 5.6 copy-start.4
  323.7 14.7 %all-to-all-start = ((bf16[8,256,128]{2,1,0:T(8,128)(2,1)}), bf16[8,256,128]{2,1,0:T(8,128)(2,1)S(1)}, u32[]{:S(2)}, u32[]{:S(2)}) async-start(bf16[8,256,128]{2,1,0:T(8,128)(2,1)} %stack.2), calls=%async_computation.1 | async-start | bytes 1048576 | tf_op jit(solution)/shard_map/all_to_all | solution.py:129
  328.3 347.8 %reduce-scatter.5.cloned.1.call-start = ((), (), s32[]{:S(2)}) async-start(), calls=%async_computation.4 | async-start | bytes 221184 | tf_op jit(solution)/shard_map/reduce_scatter | solution.py:104
  341.7 5.3 copy-start.1
  341.7 5.4 copy-start.2
  341.7 5.5 copy-start.6
  341.7 6.1 collective-permute-start
  345.2 5.7 collective-permute-start.1
  347.3 3.7 copy-start.8
  351.0 51.8 %copy-start.5 = (bf16[128,16]{0,1:T(8,128)(2,1)S(1)}, bf16[128,16]{0,1:T(8,128)(2,1)}, u32[]{:S(2)}) copy-start(bf16[128,16]{0,1:T(8,128)(2,1)} %param.34) | copy-start | bytes 12292
  559.6 117.8 %copy-start.9 = (f32[16,128]{1,0:T(8,128)S(1)}, f32[16,128]{1,0:T(8,128)}, u32[]{:S(2)}) copy-start(f32[16,128]{1,0:T(8,128)} %param.35) | copy-start | bytes 24580
Sparse Core Ops, SparseCore 0:
  246.0 75.5 reduce-scatter.2
  604.1 71.9 reduce-scatter.4
